TPU v7x, 256 devices: a whole 4x4x8 slice. The times are simulated.
256 devices in a mesh: row: 16 (over z, core), col: 16 (over x, y).
Axes of the slice: x: 4, y: 4, z: 8, core: 2. Of those that a mesh axis runs over, the one named last changes fastest.
Arguments:
- tensor: float32 [12, 8192, 8192], P(None, 'row', 'col'), may hold values from -6 to 6
- factor_b: float32 [8192, 128], P(('col', 'row')), may hold values from -0.0625 to 0.0625
- factor_c: float32 [12, 128], replicated, may hold values from -1.75 to 1.75
Outputs:
- a_update: float32 [8192, 128], P(('row', 'col'))
- b_update: float32 [8192, 128], P(('col', 'row'))
All inputs are finite; a program needn't handle non-finite values.
Results may differ from a plain program's by a relative error of at most 0.00012.
Values sent between devices are 32-bit elements; how exact they have to be, the bound alone decides.
No kernel may reach another device: no remote copies, remote signals or barrier semaphores. Data moves between devices by JAX's collectives and lax.ppermute only.
A program may use at most 64 MiB of HBM per device.

v0:
```python
import jax
import jax.numpy as jnp
from jax import lax
from jax.sharding import PartitionSpec as P

EPSILON = 1e-06


def solve_system(rhs, system):
    highest = lax.Precision.HIGHEST
    lower = jnp.linalg.cholesky(system)
    inverse = jax.scipy.linalg.cho_solve(
        (lower, True), jnp.eye(system.shape[0], dtype=system.dtype)
    )
    return jnp.dot(rhs, inverse, precision=highest)


def gram_of(matrix):
    return jnp.dot(matrix.T, matrix, precision=lax.Precision.HIGHEST)


def per_device(tensor, factor_b, factor_c):
    highest = lax.Precision.HIGHEST
    rows_block = tensor.shape[1]
    cols_block = tensor.shape[2]
    rank_width = factor_c.shape[1]
    owned_a = rows_block // lax.axis_size("col")
    owned_b = cols_block // lax.axis_size("row")
    c_gram = gram_of(factor_c)
    empty_b = jnp.zeros((cols_block, rank_width), jnp.float32)
    gram_b = lax.psum(gram_of(factor_b), ("row", "col"))
    block = tensor
    khatri = factor_c[:, None, :] * lax.all_gather(factor_b, "row", axis=0, tiled=True)[None, :, :]
    partial_a = jnp.einsum("kij,kjr->ir", block, khatri, precision=highest)
    whole_a = lax.psum(partial_a, "col")
    summed_a = lax.dynamic_slice_in_dim(whole_a, lax.axis_index("col") * owned_a, owned_a, 0)
    a_update = solve_system(summed_a, c_gram * gram_b)
    squares = lax.psum(jnp.sum(a_update * a_update, axis=0), ("row", "col"))
    factor_a = a_update / jnp.sqrt(squares + EPSILON)
    gram_a = lax.psum(gram_of(factor_a), ("row", "col"))
    block = tensor
    khatri = factor_c[:, None, :] * lax.all_gather(factor_a, "col", axis=0, tiled=True)[None, :, :]
    partial_b = empty_b + jnp.einsum("kij,kir->jr", block, khatri, precision=highest)
    whole_b = lax.psum(partial_b, "row")
    summed_b = lax.dynamic_slice_in_dim(whole_b, lax.axis_index("row") * owned_b, owned_b, 0)
    b_update = solve_system(summed_b, c_gram * gram_a)
    return (a_update, b_update)


def solution(mesh):
    placed = (P(None, "row", "col"), P(("col", "row"), None), P())
    return jax.shard_map(
        per_device,
        mesh=mesh,
        in_specs=placed,
        out_specs=(P(("row", "col"), None), P(("col", "row"), None)),
        check_vma=False,
    )
```

profile of v0, /device:TPU:1, one launch (start us, length us, event | category | flops | bytes accessed | tf_op | source)
XLA Modules:
  0.0 809.7 jit_solution(5450451104905007428)
XLA Ops:
  7.2 1.7 fusion.35
  9.0 22.3 %all_gather.6 = f32[512,128]{1,0:T(8,128)S(1)} all-gather(f32[32,128]{1,0:T(8,128)} %param.7), channel_id=1, replica_groups=mesh['row'=16,'col'=16] {'row'}, dimensions={0}, use_global_device_ids=true | all-gather | bytes 278528 | tf_op jit(solution)/shard_map/all_gather | solution.py:33
  31.2 18.3 %fusion.8 = f32[512,128]{0,1:T(8,128)} fusion(f32[12,512,512]{2,1,0:T(8,128)} %param.6, f32[512,128]{1,0:T(8,128)S(1)} %all_gather.6, f32[12,128]{1,0:T(8,128)} %param.8), kind=kOutput, calls=%fused_computation.8 | convolution fusion | flops 4832624640 | bytes 13113344 | tf_op jit(solution)/shard_map/kij,kjr->ir/dot_general | solution.py:34
  49.8 209.2 %all-reduce.7.cloned.1.call-done = f32[128,128]{0,1:T(8,128)} async-done(((f32[128,128]{0,1:T(8,128)}), f32[128,128]{0,1:T(8,128)}) %all-reduce.7.cloned.1.call-update) | async-done | bytes 65552 | tf_op jit(solution)/shard_map/psum | solution.py:31
  259.1 1.1 fusion.34
  260.3 11.7 %cholesky.44 = f32[128,128]{1,0:T(8,128)S(1)} custom-call(f32[128,128]{1,0:T(8,128)S(1)} %fusion.27), custom_call_target="Cholesky" | custom-call | tf_op jit(solution)/shard_map/jit(cholesky)/cholesky | solution.py:11
  272.1 0.6 compare_reduce_fusion.1
  272.7 0.7 fusion.18
  273.4 9.8 %custom-call.8 = f32[1,128,128]{1,2,0:T(8,128)S(1)} custom-call(f32[1,128,128]{2,1,0:T(8,128)S(1)} %fusion.18), custom_call_target="InvertDiagBlocksLowerTriangular" | custom-call | tf_op jit(solution)/shard_map/jit(_cho_solve)/triangular_solve | solution.py:12
  283.2 0.3 fusion.16
  283.7 68.0 %all-reduce.5.cloned.1.call-done = f32[512,128]{0,1:T(8,128)} async-done(((f32[512,128]{0,1:T(8,128)}), f32[512,128]{0,1:T(8,128)}) %all-reduce.5.cloned.1.call-update) | async-done | bytes 262160 | tf_op jit(solution)/shard_map/psum | solution.py:35
  351.7 1.2 multiply_reduce_fusion
  352.8 77.5 %psum.37 = f32[128]{0:T(128)S(1)} all-reduce(f32[128]{0:T(128)S(1)} %get-tuple-element.6), channel_id=1, replica_groups=mesh['row'=16,'col'=16] {'row','col'}, use_global_device_ids=true, to_apply=%region_5.0 | all-reduce | flops 128 | bytes 1024 | tf_op jit(solution)/shard_map/psum | solution.py:38
  430.3 0.9 fusion.36
  431.3 15.8 %all_gather.7 = f32[512,128]{1,0:T(8,128)S(1)} all-gather(f32[32,128]{1,0:T(8,128)S(1)} %broadcast_divide_fusion), channel_id=1, replica_groups=mesh['row'=16,'col'=16] {'col'}, dimensions={0}, use_global_device_ids=true | all-gather | bytes 278528 | tf_op jit(solution)/shard_map/all_gather | solution.py:42
  447.3 11.4 %fusion.11 = f32[512,128]{0,1:T(8,128)} fusion(f32[12,512,512]{2,1,0:T(8,128)} %param.6, f32[512,128]{1,0:T(8,128)S(1)} %all_gather.7, f32[12,128]{1,0:T(8,128)S(1)} %copy-done), kind=kOutput, calls=%fused_computation.9 | convolution fusion | flops 4832624640 | bytes 13113344 | tf_op jit(solution)/shard_map/kij,kir->jr/dot_general | solution.py:43
  458.8 234.0 %all-reduce.11.cloned.1.call-done = f32[128,128]{0,1:T(8,128)} async-done(((f32[128,128]{0,1:T(8,128)}), f32[128,128]{0,1:T(8,128)}) %all-reduce.11.cloned.1.call-update) | async-done | bytes 65552 | tf_op jit(solution)/shard_map/psum | solution.py:40
  692.8 0.9 mul.48
  693.8 11.7 %cholesky.55 = f32[128,128]{1,0:T(8,128)S(1)} custom-call(f32[128,128]{1,0:T(8,128)S(1)} %fusion.23), custom_call_target="Cholesky" | custom-call | tf_op jit(solution)/shard_map/jit(cholesky)/cholesky | solution.py:11
  705.5 0.6 compare_reduce_fusion
  706.2 0.7 fusion.19
  706.8 9.8 %custom-call.9 = f32[1,128,128]{1,2,0:T(8,128)S(1)} custom-call(f32[1,128,128]{2,1,0:T(8,128)S(1)} %fusion.19), custom_call_target="InvertDiagBlocksLowerTriangular" | custom-call | tf_op jit(solution)/shard_map/jit(_cho_solve)/triangular_solve | solution.py:12
  717.2 84.3 %all-reduce.9.cloned.1.call-done = f32[512,128]{0,1:T(8,128)} async-done(((f32[512,128]{0,1:T(8,128)}), f32[512,128]{0,1:T(8,128)}) %all-reduce.9.cloned.1.call-update) | async-done | bytes 262160 | tf_op jit(solution)/shard_map/psum | solution.py:44
  801.4 1.8 fusion.28
  (23 shorter events, 1.6 us)
Async XLA Ops:
  7.2 251.9 %all-reduce.7.cloned.1.call-start = ((), (), s32[]{:S(2)}) async-start(), calls=%async_computation.1 | async-start | bytes 131072 | tf_op jit(solution)/shard_map/psum | solution.py:31
  8.9 342.7 %all-reduce.5.cloned.1.call-start = ((), (), s32[]{:S(2)}) async-start(), calls=%async_computation | async-start | bytes 524288 | tf_op jit(solution)/shard_map/psum | solution.py:35
  31.2 227.8 %copy-start = (f32[12,128]{1,0:T(8,128)S(1)}, f32[12,128]{1,0:T(8,128)}, u32[]{:S(2)}) copy-start(f32[12,128]{1,0:T(8,128)} %param.8) | copy-start | bytes 18436
  49.6 643.2 %all-reduce.11.cloned.1.call-start = ((), (), s32[]{:S(2)}) async-start(), calls=%async_computation.3 | async-start | bytes 131072 | tf_op jit(solution)/shard_map/psum | solution.py:40
  352.8 105.9 %copy-start.1 = (f32[32,128]{1,0:T(8,128)}, f32[32,128]{1,0:T(8,128)S(1)}, u32[]{:S(2)}) copy-start(f32[32,128]{1,0:T(8,128)S(1)} %get-tuple-element.7) | copy-start | bytes 49156
  447.1 354.4 %all-reduce.9.cloned.1.call-start = ((), (), s32[]{:S(2)}) async-start(), calls=%async_computation.2 | async-start | bytes 524288 | tf_op jit(solution)/shard_map/psum | solution.py:44
Sparse Core Ops, SparseCore 0:
  13.5 245.5 all-reduce.6
  262.2 89.3 all-reduce.4
  447.2 245.5 all-reduce.10
  695.0 106.4 all-reduce.8
where the time goes:
time: 810 us
  waiting for transfers between devices  596 us (74%)
  blocking collectives  116 us (14%)
  other arithmetic  46.6 us (6%)
  matrix products  37.4 us (5%)
  between operations  13.9 us (2%)
    psum x1, waiting for transfers between devices, per_device(): gram_a = lax.psum(gram_of(factor_a), ('row', 'col'))  234 us
    psum x1, waiting for transfers between devices, per_device(): gram_b = lax.psum(gram_of(factor_b), ('row', 'col'))  209 us
    psum x1, waiting for transfers between devices, per_device(): whole_b = lax.psum(partial_b, 'row')  84.3 us
    psum x1, blocking collectives, per_device(): squares = lax.psum(jnp.sum(a_update * a_update, axis=0), ('row', 'col'))  77.5 us
    psum x1, waiting for transfers between devices, per_device(): whole_a = lax.psum(partial_a, 'col')  68 us
    another operation x6, other arithmetic, solve_system(): lower = jnp.linalg.cholesky(system)  24.8 us
    all_gather x1, blocking collectives, per_device(): lax.all_gather(factor_b, 'row', axis=0, tiled=True)[None, :, :]  22.3 us
    another operation x4, other arithmetic, solve_system(): jax.scipy.linalg.cho_solve((lower, True), jnp.eye(system.shape[0], dtype=...  20.9 us
  transfers between devices with their start and end apart: 4, of which 4 were waited for; matrix products, arithmetic and copies ran while one was open for 10% of the time, Pallas kernels for 0%

commit v1 on v0

--- a/solution.py
+++ b/solution.py
@@ -28,7 +28,7 @@
     owned_b = cols_block // lax.axis_size("row")
     c_gram = gram_of(factor_c)
     empty_b = jnp.zeros((cols_block, rank_width), jnp.float32)
-    gram_b = lax.psum(gram_of(factor_b), ("row", "col"))
+    gram_b = lax.psum(lax.psum(gram_of(factor_b), "row"), "col")
     block = tensor
     khatri = factor_c[:, None, :] * lax.all_gather(factor_b, "row", axis=0, tiled=True)[None, :, :]
     partial_a = jnp.einsum("kij,kjr->ir", block, khatri, precision=highest)

time: 810 us -> 692 us (0.85)
  waiting for transfers between devices: 596 us -> 477 us
    psum x2, waiting for transfers between devices: 277 us -> 159 us  [per_device(): gram_b = lax.psum(lax.psum(gram_of(factor_b), 'row'), 'col')]
  transfers between devices with their start and end apart: 4 -> 4, of which waited for: 4 -> 4; matrix products, arithmetic and copies ran while one was open for 10% -> 8% of each run, Pallas kernels for 0% -> 0%
where the time goes in v1:
time: 692 us
  waiting for transfers between devices  477 us (69%)
  blocking collectives  116 us (17%)
  other arithmetic  46.6 us (7%)
  matrix products  37.5 us (5%)
  between operations  13.9 us (2%)
    psum x1, waiting for transfers between devices, per_device(): gram_a = lax.psum(gram_of(factor_a), ('row', 'col'))  234 us
    psum x2, waiting for transfers between devices, per_device(): gram_b = lax.psum(lax.psum(gram_of(factor_b), 'row'), 'col')  159 us
    psum x1, waiting for transfers between devices, per_device(): whole_b = lax.psum(partial_b, 'row')  84.3 us
    psum x1, blocking collectives, per_device(): squares = lax.psum(jnp.sum(a_update * a_update, axis=0), ('row', 'col'))  77.5 us
    another operation x6, other arithmetic, solve_system(): lower = jnp.linalg.cholesky(system)  24.8 us
    all_gather x1, blocking collectives, per_device(): lax.all_gather(factor_b, 'row', axis=0, tiled=True)[None, :, :]  22.3 us
    another operation x4, other arithmetic, solve_system(): jax.scipy.linalg.cho_solve((lower, True), jnp.eye(system.shape[0], dtype=...  20.9 us
    dot_general x1, matrix products, per_device(): partial_a = jnp.einsum('kij,kjr->ir', block, khatri, precision=highest)  18.3 us
  transfers between devices with their start and end apart: 4, of which 4 were waited for; matrix products, arithmetic and copies ran while one was open for 8% of the time, Pallas kernels for 0%

profile of v1, /device:TPU:1, one launch (start us, length us, event | category | flops | bytes accessed | tf_op | source)
XLA Modules:
  0.0 691.6 jit_solution(11037113532238475073)
XLA Ops:
  7.2 1.7 fusion.35
  9.0 22.3 %all_gather.6 = f32[512,128]{1,0:T(8,128)S(1)} all-gather(f32[32,128]{1,0:T(8,128)} %param.7), channel_id=1, replica_groups=mesh['row'=16,'col'=16] {'row'}, dimensions={0}, use_global_device_ids=true | all-gather | bytes 278528 | tf_op jit(solution)/shard_map/all_gather | solution.py:33
  31.2 18.3 %fusion.8 = f32[512,128]{0,1:T(8,128)} fusion(f32[12,512,512]{2,1,0:T(8,128)} %param.6, f32[512,128]{1,0:T(8,128)S(1)} %all_gather.6, f32[12,128]{1,0:T(8,128)} %param.8), kind=kOutput, calls=%fused_computation.8 | convolution fusion | flops 4832624640 | bytes 13113344 | tf_op jit(solution)/shard_map/kij,kjr->ir/dot_general | solution.py:34
  49.6 65.4 %all-reduce.6.cloned.1.call-done = f32[128,128]{0,1:T(8,128)} async-done(((f32[128,128]{0,1:T(8,128)}), f32[128,128]{0,1:T(8,128)}) %all-reduce.6.cloned.1.call-update) | async-done | bytes 65552 | tf_op jit(solution)/shard_map/psum | solution.py:31
  115.2 93.7 %all-reduce.12.cloned.1.call-done = (f32[128,128]{0,1:T(8,128)}, f32[512,128]{0,1:T(8,128)}) async-done(((f32[128,128]{0,1:T(8,128)}, f32[512,128]{0,1:T(8,128)}), (f32[128,128]{0,1:T(8,128)}, f32[512,128]{0,1:T(8,128)})) %all-reduce.12.cloned.1.call-update) | async-done | bytes 327696 | tf_op jit(solution)/shard_map/psum | solution.py:31
  208.9 1.1 fusion.34
  210.1 11.7 %cholesky.44 = f32[128,128]{1,0:T(8,128)S(1)} custom-call(f32[128,128]{1,0:T(8,128)S(1)} %fusion.27), custom_call_target="Cholesky" | custom-call | tf_op jit(solution)/shard_map/jit(cholesky)/cholesky | solution.py:11
  221.9 0.6 compare_reduce_fusion.1
  222.5 0.7 fusion.18
  223.2 9.8 %custom-call.8 = f32[1,128,128]{1,2,0:T(8,128)S(1)} custom-call(f32[1,128,128]{2,1,0:T(8,128)S(1)} %fusion.18), custom_call_target="InvertDiagBlocksLowerTriangular" | custom-call | tf_op jit(solution)/shard_map/jit(_cho_solve)/triangular_solve | solution.py:12
  233.5 1.2 multiply_reduce_fusion
  234.7 77.5 %psum.45 = f32[128]{0:T(128)S(1)} all-reduce(f32[128]{0:T(128)S(1)} %get-tuple-element.8), channel_id=1, replica_groups=mesh['row'=16,'col'=16] {'row','col'}, use_global_device_ids=true, to_apply=%region_6.0 | all-reduce | flops 128 | bytes 1024 | tf_op jit(solution)/shard_map/psum | solution.py:38
  312.2 0.9 fusion.36
  313.1 15.8 %all_gather.7 = f32[512,128]{1,0:T(8,128)S(1)} all-gather(f32[32,128]{1,0:T(8,128)S(1)} %broadcast_divide_fusion), channel_id=1, replica_groups=mesh['row'=16,'col'=16] {'col'}, dimensions={0}, use_global_device_ids=true | all-gather | bytes 278528 | tf_op jit(solution)/shard_map/all_gather | solution.py:42
  329.2 11.4 %fusion.11 = f32[512,128]{0,1:T(8,128)} fusion(f32[12,512,512]{2,1,0:T(8,128)} %param.6, f32[512,128]{1,0:T(8,128)S(1)} %all_gather.7, f32[12,128]{1,0:T(8,128)S(1)} %copy-done), kind=kOutput, calls=%fused_computation.9 | convolution fusion | flops 4832624640 | bytes 13113344 | tf_op jit(solution)/shard_map/kij,kir->jr/dot_general | solution.py:43
  340.7 234.0 %all-reduce.10.cloned.1.call-done = f32[128,128]{0,1:T(8,128)} async-done(((f32[128,128]{0,1:T(8,128)}), f32[128,128]{0,1:T(8,128)}) %all-reduce.10.cloned.1.call-update) | async-done | bytes 65552 | tf_op jit(solution)/shard_map/psum | solution.py:40
  574.7 0.8 mul.48
  575.6 11.7 %cholesky.55 = f32[128,128]{1,0:T(8,128)S(1)} custom-call(f32[128,128]{1,0:T(8,128)S(1)} %fusion.23), custom_call_target="Cholesky" | custom-call | tf_op jit(solution)/shard_map/jit(cholesky)/cholesky | solution.py:11
  587.4 0.6 compare_reduce_fusion
  588.0 0.7 fusion.19
  588.7 9.8 %custom-call.9 = f32[1,128,128]{1,2,0:T(8,128)S(1)} custom-call(f32[1,128,128]{2,1,0:T(8,128)S(1)} %fusion.19), custom_call_target="InvertDiagBlocksLowerTriangular" | custom-call | tf_op jit(solution)/shard_map/jit(_cho_solve)/triangular_solve | solution.py:12
  598.5 0.3 fusion.14
  599.0 84.3 %all-reduce.8.cloned.1.call-done = f32[512,128]{0,1:T(8,128)} async-done(((f32[512,128]{0,1:T(8,128)}), f32[512,128]{0,1:T(8,128)}) %all-reduce.8.cloned.1.call-update) | async-done | bytes 262160 | tf_op jit(solution)/shard_map/psum | solution.py:44
  683.3 1.8 fusion.28
  (23 shorter events, 1.6 us)
Async XLA Ops:
  7.2 107.8 %all-reduce.6.cloned.1.call-start = ((), (), s32[]{:S(2)}) async-start(), calls=%async_computation | async-start | bytes 131072 | tf_op jit(solution)/shard_map/psum | solution.py:31
  8.9 199.9 %all-reduce.12.cloned.1.call-start = ((), (), s32[]{:S(2)}) async-start(), calls=%async_computation.3 | async-start | bytes 655360 | tf_op jit(solution)/shard_map/psum | solution.py:31
  31.2 177.6 %copy-start = (f32[12,128]{1,0:T(8,128)S(1)}, f32[12,128]{1,0:T(8,128)}, u32[]{:S(2)}) copy-start(f32[12,128]{1,0:T(8,128)} %param.8) | copy-start | bytes 18436
  115.0 459.7 %all-reduce.10.cloned.1.call-start = ((), (), s32[]{:S(2)}) async-start(), calls=%async_computation.2 | async-start | bytes 131072 | tf_op jit(solution)/shard_map/psum | solution.py:40
  234.7 106.0 %copy-start.1 = (f32[32,128]{1,0:T(8,128)}, f32[32,128]{1,0:T(8,128)S(1)}, u32[]{:S(2)}) copy-start(f32[32,128]{1,0:T(8,128)S(1)} %get-tuple-element.9) | copy-start | bytes 49156
  328.9 354.4 %all-reduce.8.cloned.1.call-start = ((), (), s32[]{:S(2)}) async-start(), calls=%async_computation.1 | async-start | bytes 524288 | tf_op jit(solution)/shard_map/psum | solution.py:44
Sparse Core Ops, SparseCore 0:
  10.3 104.6 all-reduce.5
  118.2 90.5 all-reduce.11
  329.1 245.5 all-reduce.9
  576.8 106.3 all-reduce.7
